TPU v7x, 32 devices: a whole 2x2x4 slice. The times are simulated.
32 devices in a mesh: row: 8 (over y, x, core), col: 4 (over z).
Axes of the slice: x: 2, y: 2, z: 4, core: 2. Of those that a mesh axis runs over, the one named last changes fastest.
Arguments:
- density: bfloat16 [4096, 4096], P('row', 'col'), as said below
- pattern: int32 [64, 64], P('row', 'col'), may hold values from 0 to 1, as said below
Outputs:
- updated: bfloat16 [4096, 4096], P('row', 'col')
- occupations: float32 [2], replicated
Inputs may be any that keep to these rules, and one draw needn't show every extreme that they name: pattern is symmetric, every diagonal block is 1. density is exactly symmetric and zero wherever pattern is 0.
All inputs are finite; a program needn't handle non-finite values.
Results may differ from a plain program's by a relative error of at most 0.0015.
Values may be sent and summed in bfloat16 or wider, within the bound.
A program may use at most 64 MiB of HBM per device.

v0:
```python
import jax
import jax.numpy as jnp
from jax import lax
from jax.sharding import PartitionSpec as P

BLK = 64


def expand_blocks(block_mask, width):
    block_rows, block_cols = block_mask.shape
    grid = jnp.broadcast_to(
        block_mask.astype(jnp.float32)[:, None, :, None], (block_rows, width, block_cols, width)
    )
    return grid.reshape(block_rows * width, block_cols * width)


def body(density, pattern):
    slab_rows, slab_cols = density.shape
    cell_mask = expand_blocks(pattern, BLK)
    column_panel = lax.all_gather(density, "row", axis=0, tiled=True)
    row_offset = lax.axis_index("row") * slab_rows
    col_offset = lax.axis_index("col") * slab_cols
    global_rows = row_offset + lax.iota(jnp.int32, slab_rows)
    global_cols = col_offset + lax.iota(jnp.int32, slab_cols)
    on_diagonal = global_rows[:, None] == global_cols[None, :]
    density_wide = density.astype(jnp.float32)
    trace_p_part = jnp.sum(jnp.where(on_diagonal, density_wide, 0.0))
    square = jnp.dot(
        lax.all_gather(density, "col", axis=1, tiled=True),
        column_panel,
        preferred_element_type=jnp.float32,
    )
    square = square * cell_mask
    trace_c_part = jnp.sum(jnp.where(on_diagonal, square, 0.0))
    trace_p, trace_c = lax.psum((trace_p_part, trace_c_part), ("row", "col"))
    order_total = slab_rows * lax.axis_size("row")
    take_square = trace_p > 1.0 * order_total
    updated = jnp.where(take_square, square, cell_mask * (2.0 * density_wide - square))
    trace_new = jnp.where(take_square, trace_c, 2.0 * trace_p - trace_c)
    occupations = jnp.stack([trace_p, trace_new]) / order_total
    return (updated.astype(jnp.bfloat16), occupations)


def solution(mesh):
    placed = (P("row", "col"), P("row", "col"))
    return jax.shard_map(
        body, mesh=mesh, in_specs=placed, out_specs=(P("row", "col"), P()), check_vma=False
    )
```

profile of v0, /device:TPU:0, one launch (start us, length us, event | category | flops | bytes accessed | tf_op | source)
XLA Modules:
  0.0 212.4 jit_solution(5599611315656936817)
XLA Ops:
  7.2 0.0 copy-start.1
  7.2 0.0 all-gather.3.cloned.1.call-start
  7.2 0.7 all-gather.3.cloned.1.call-update
  7.9 0.0 all-gather.5.cloned.1.call-start
  8.0 0.7 all-gather.5.cloned.1.call-update
  8.7 0.0 copy-done.1
  8.7 2.3 %broadcast_in_dim.14 = f32[8,64,16,64]{3,2,1,0:T(8,128)} broadcast(f32[8,16]{1,0:T(8,128)S(1)} %convert_element_type.10), dimensions={0,2} | broadcast | bytes 2097664 | tf_op jit(solution)/shard_map/broadcast_in_dim | solution.py:11
  11.0 0.0 copy-start
  11.0 3.6 %reshape.16 = f32[512,1024]{1,0:T(8,128)S(1)} reshape(f32[8,64,16,64]{3,2,1,0:T(8,128)} %broadcast_in_dim.14) | data formatting | bytes 4194304 | tf_op jit(solution)/shard_map/reshape | solution.py:14
  14.6 78.5 %all-gather.3.cloned.1.call-done = bf16[512,4096]{1,0:T(8,128)(2,1)} async-done(((bf16[512,1024]{1,0:T(8,128)(2,1)}), bf16[512,4096]{1,0:T(8,128)(2,1)}) %all-gather.3.cloned.1.call-update) | async-done | bytes 4194320 | tf_op jit(solution)/shard_map/all_gather | solution.py:29
  93.1 54.8 %all-gather.5.cloned.1.call-done = bf16[4096,1024]{1,0:T(8,128)(2,1)} async-done(((bf16[512,1024]{1,0:T(8,128)(2,1)}), bf16[4096,1024]{1,0:T(8,128)(2,1)}) %all-gather.5.cloned.1.call-update) | async-done | bytes 8388624 | tf_op jit(solution)/shard_map/all_gather | solution.py:20
  147.9 0.0 copy-done
  147.9 11.1 %fusion.5 = (f32[]{:T(128)}, f32[]{:T(128)}, f32[512,1024]{1,0:T(8,128)}) fusion(f32[512,1024]{1,0:T(8,128)S(1)} %reshape.16, s32[1024]{0:T(1024)S(1)} %iota_add_fusion, s32[512]{0:T(512)S(1)} %iota_add_fusion.1, bf16[512,1024]{1,0:T(8,128)(2,1)S(1)} %copy-done, bf16[512,4096]{1,0:T(8,128)(2,1)} %all-gather.3.cloned.1.call-done, ...), kind=kOutput, calls=%fused_computation.8 | convolution fusion | flops 4298637312 | bytes 17831944 | tf_op jit(solution)/shard_map/dot_general | solution.py:28
  159.0 39.6 %all-reduce = (f32[]{:T(128)}, f32[]{:T(128)}) all-reduce(f32[]{:T(128)} %get-tuple-element.3, f32[]{:T(128)} %get-tuple-element.2), channel_id=1, replica_groups=mesh['row'=8,'col'=4] {'row','col'}, use_global_device_ids=true, to_apply=%region_1.2 | all-reduce | flops 2 | bytes 16 | tf_op jit(solution)/shard_map/psum | solution.py:35
  201.2 3.2 %fusion.3 = bf16[512,1024]{1,0:T(8,128)(2,1)} fusion(f32[512,1024]{1,0:T(8,128)S(1)} %reshape.16, bf16[512,1024]{1,0:T(8,128)(2,1)S(1)} %copy-done, f32[512,1024]{1,0:T(8,128)} %get-tuple-element.6, pred[]{:T(512)S(6)} %gt.3), kind=kLoop, calls=%fused_computation.6 | loop fusion | flops 3670016 | bytes 6291457 | tf_op jit(solution)/shard_map/convert_element_type | solution.py:41
  204.3 1.2 maximum_multiply_fusion
  (3 shorter events, 0.0 us)
Async XLA Ops:
  7.2 1.5 copy-start.1
  7.2 85.9 %all-gather.3.cloned.1.call-start = ((), (), s32[]{:S(2)}) async-start(), calls=%async_computation | async-start | bytes 5242880 | tf_op jit(solution)/shard_map/all_gather | solution.py:29
  7.9 140.0 %all-gather.5.cloned.1.call-start = ((), (), s32[]{:S(2)}) async-start(), calls=%async_computation.1 | async-start | bytes 9437184 | tf_op jit(solution)/shard_map/all_gather | solution.py:20
  11.0 136.9 %copy-start = (bf16[512,1024]{1,0:T(8,128)(2,1)S(1)}, bf16[512,1024]{1,0:T(8,128)(2,1)}, u32[]{:S(2)}) copy-start(bf16[512,1024]{1,0:T(8,128)(2,1)} %param.2) | copy-start | bytes 3145732
Sparse Core Ops, SparseCore 0:
  9.6 83.4 all-gather.2
  95.0 52.9 all-gather.4
where the time goes:
time: 213 us; the launch traced here: 212 us
  waiting for transfers between devices  135 us (63%)
  blocking collectives  39.6 us (19%)
  between operations  16.7 us (8%)
  matrix products  11.1 us (5%)
  local copies, waits for them, and re-layouts  5.88 us (3%)
  other arithmetic  4.4 us (2%)
    all_gather x1, waiting for transfers between devices, body(): lax.all_gather(density, 'col', axis=1, tiled=True)  78.5 us
    all_gather x1, waiting for transfers between devices, body(): column_panel = lax.all_gather(density, 'row', axis=0, tiled=True)  54.8 us
    psum x1, blocking collectives, body(): trace_p, trace_c = lax.psum((trace_p_part, trace_c_part), ('row', 'col'))  39.6 us
    dot_general x1, matrix products, body(): jnp.dot(lax.all_gather(density, 'col', axis=1, tiled=True), column_panel,...  11.1 us
  transfers between devices with their start and end apart: 2, of which 2 were waited for; matrix products, arithmetic and copies ran while one was open for 3% of the time, Pallas kernels for 0%

commit v1 on v0

--- a/solution.py
+++ b/solution.py
@@ -4,6 +4,27 @@
 from jax.sharding import PartitionSpec as P
 
 BLK = 64
+
+
+def joined_along(blocks, dim):
+    blocks = jnp.moveaxis(blocks, 0, dim)
+    dims = blocks.shape
+    return blocks.reshape(*dims[:dim], dims[dim] * dims[dim + 1], *dims[dim + 2 :])
+
+
+def grow_blocks(value, axis):
+    devices, index = (lax.axis_size(axis), lax.axis_index(axis))
+    blocks, bit = (value[None], 1)
+    while bit < devices:
+        other = lax.ppermute(blocks, axis, [(i, i ^ bit) for i in range(devices)])
+        low = index & bit == 0
+        blocks = jnp.concatenate([jnp.where(low, blocks, other), jnp.where(low, other, blocks)])
+        bit *= 2
+    return blocks
+
+
+def doubled_up(x, axis, dim):
+    return joined_along(grow_blocks(x, axis), dim)
 
 
 def expand_blocks(block_mask, width):
@@ -26,9 +47,7 @@
     density_wide = density.astype(jnp.float32)
     trace_p_part = jnp.sum(jnp.where(on_diagonal, density_wide, 0.0))
     square = jnp.dot(
-        lax.all_gather(density, "col", axis=1, tiled=True),
-        column_panel,
-        preferred_element_type=jnp.float32,
+        doubled_up(density, "col", 1), column_panel, preferred_element_type=jnp.float32
     )
     square = square * cell_mask
     trace_c_part = jnp.sum(jnp.where(on_diagonal, square, 0.0))

time: 213 us -> 202 us (0.948)
  waiting for transfers between devices: 135 us -> 107 us
  other arithmetic: 4.4 us -> 11.5 us
  starting transfers between devices: 0.08 us -> 5.88 us
  local copies, waits for them, and re-layouts: 5.88 us -> 9.49 us
    ppermute x0 -> x2, waiting for transfers between devices: none -> 106 us  [grow_blocks(): other = lax.ppermute(blocks, axis, [(i, i ^ bit) for i in range(devices)])]
    all_gather x1 -> x0, waiting for transfers between devices: 78.5 us -> none  [body(): lax.all_gather(density, 'col', axis=1, tiled=True)]
    all_gather x1, waiting for transfers between devices: 54.8 us -> 0.01 us  [body(): column_panel = lax.all_gather(density, 'row', axis=0, tiled=True)]
    ppermute x0 -> x2, starting transfers between devices: none -> 5.84 us  [grow_blocks(): other = lax.ppermute(blocks, axis, [(i, i ^ bit) for i in range(devices)])]
    concatenate x0 -> x2, other arithmetic: none -> 3.93 us  [grow_blocks(): jnp.concatenate([jnp.where(low, blocks, other), jnp.where(low, other, blo...]
    select_n x0 -> x2, other arithmetic: none -> 3.23 us  [grow_blocks(): jnp.where(low, blocks, other)]
    unnamed x4 -> x7, local copies, waits for them, and re-layouts: 0.01 us -> 2.35 us
  transfers between devices with their start and end apart: 2 -> 3, of which waited for: 2 -> 2; matrix products, arithmetic and copies ran while one was open for 3% -> 8% of each run, Pallas kernels for 0% -> 0%
where the time goes in v1:
time: 202 us; the launch traced here: 201 us
  waiting for transfers between devices  107 us (53%)
  blocking collectives  39.9 us (20%)
  between operations  16.6 us (8%)
  other arithmetic  11.5 us (6%)
  matrix products  11.1 us (5%)
  local copies, waits for them, and re-layouts  9.49 us (5%)
  starting transfers between devices  5.88 us (3%)
    ppermute x2, waiting for transfers between devices, grow_blocks(): other = lax.ppermute(blocks, axis, [(i, i ^ bit) for i in range(devices)])  106 us
    psum x1, blocking collectives, body(): trace_p, trace_c = lax.psum((trace_p_part, trace_c_part), ('row', 'col'))  39.9 us
    dot_general x1, matrix products, body(): jnp.dot(doubled_up(density, 'col', 1), column_panel, preferred_element_ty...  11.1 us
    ppermute x2, starting transfers between devices, grow_blocks(): other = lax.ppermute(blocks, axis, [(i, i ^ bit) for i in range(devices)])  5.84 us
    reshape x1, local copies, waits for them, and re-layouts, expand_blocks(): return grid.reshape(block_rows * width, block_cols * width)  4.85 us
  transfers between devices with their start and end apart: 3, of which 2 were waited for; matrix products, arithmetic and copies ran while one was open for 8% of the time, Pallas kernels for 0%

profile of v1, /device:TPU:0, one launch (start us, length us, event | category | flops | bytes accessed | tf_op | source)
XLA Modules:
  0.0 201.5 jit_solution(17020744679432661704)
XLA Ops:
  7.2 0.0 all-gather.2.cloned.1.call-start
  7.2 0.7 all-gather.2.cloned.1.call-update
  7.9 1.5 copy.4
  9.4 3.1 %collective-permute-start = (bf16[1,512,1024]{1,2,0:T(8,128)(2,1)S(1)}, bf16[1,512,1024]{1,2,0:T(8,128)(2,1)}, u32[]{:S(2)}, u32[]{:S(2)}) collective-permute-start(bf16[1,512,1024]{1,2,0:T(8,128)(2,1)S(1)} %bitcast.12), channel_id=1, source_target_pairs={{0,1},{1,0},{2,3},{3,2},{4,5},{5,4},{6,7},{7,6},{8,9},{9,8},{10,11... | collective-permute-start | bytes 3145736 | tf_op jit(solution)/shard_map/ppermute | solution.py:19
  12.5 23.3 %collective-permute-done = bf16[1,512,1024]{1,2,0:T(8,128)(2,1)} collective-permute-done((bf16[1,512,1024]{1,2,0:T(8,128)(2,1)S(1)}, bf16[1,512,1024]{1,2,0:T(8,128)(2,1)}, u32[]{:S(2)}, u32[]{:S(2)}) %collective-permute-start) | collective-permute-done | bytes 1048608 | tf_op jit(solution)/shard_map/ppermute | solution.py:19
  35.8 1.4 broadcast_select_fusion.3
  37.1 0.0 copy-start.2
  37.1 1.5 pad_maximum_fusion.1
  38.6 2.8 %collective-permute-start.1 = (bf16[2,512,1024]{1,2,0:T(8,128)(2,1)}, bf16[2,512,1024]{1,2,0:T(8,128)(2,1)}, u32[]{:S(2)}, u32[]{:S(2)}) collective-permute-start(bf16[2,512,1024]{1,2,0:T(8,128)(2,1)} %pad_maximum_fusion.1), channel_id=1, source_target_pairs={{0,2},{1,3},{2,0},{3,1},{4,6},{5,7},{6,4},{7,5},{8,10},{9,11},{10,... | collective-permute-start | bytes 6291464 | tf_op jit(solution)/shard_map/ppermute | solution.py:19
  41.4 0.0 copy-done.2
  41.4 2.3 %broadcast_in_dim.18 = f32[8,64,16,64]{3,2,1,0:T(8,128)} broadcast(f32[8,16]{1,0:T(8,128)S(1)} %convert_element_type.10), dimensions={0,2} | broadcast | bytes 2097664 | tf_op jit(solution)/shard_map/broadcast_in_dim | solution.py:32
  43.7 4.8 %reshape.20 = f32[512,1024]{1,0:T(8,128)} reshape(f32[8,64,16,64]{3,2,1,0:T(8,128)} %broadcast_in_dim.18) | data formatting | bytes 4194304 | tf_op jit(solution)/shard_map/reshape | solution.py:35
  48.5 83.1 %collective-permute-done.1 = bf16[2,512,1024]{1,2,0:T(8,128)(2,1)} collective-permute-done((bf16[2,512,1024]{1,2,0:T(8,128)(2,1)}, bf16[2,512,1024]{1,2,0:T(8,128)(2,1)}, u32[]{:S(2)}, u32[]{:S(2)}) %collective-permute-start.1) | collective-permute-done | bytes 2097184 | tf_op jit(solution)/shard_map/ppermute | solution.py:19
  131.6 1.9 broadcast_select_fusion.1
  133.5 0.0 copy-start
  133.5 0.0 copy-start.1
  133.5 2.4 %pad_maximum_fusion = bf16[4,512,1024]{1,2,0:T(8,128)(2,1)} fusion(bf16[2,512,1024]{1,2,0:T(8,128)(2,1)S(1)} %get-tuple-element.7, bf16[2,512,1024]{1,2,0:T(8,128)(2,1)S(1)} %get-tuple-element.6), kind=kLoop, calls=%fused_computation | loop fusion | flops 2097152 | bytes 8388608 | tf_op jit(solution)/shard_map/concatenate | solution.py:21
  135.9 0.0 all-gather.2.cloned.1.call-done
  135.9 0.0 copy-done
  135.9 0.8 copy-done.1
  136.8 11.1 %fusion.5 = (f32[]{:T(128)}, f32[]{:T(128)}, f32[512,1024]{1,0:T(8,128)}) fusion(f32[512,1024]{1,0:T(8,128)S(1)} %copy-done.1, s32[1024]{0:T(1024)S(1)} %iota_add_fusion, s32[512]{0:T(512)S(1)} %iota_add_fusion.1, bf16[512,1024]{1,0:T(8,128)(2,1)S(1)} %copy-done, bf16[512,4096]{0,1:T(8,128)(2,1)} %bitcast.13, bf16[4096,1024]{1,0:T(8,128)(2,1)} %all-gather.2.cloned.1.call-done), kind=kOutput, calls=%fused_computation.9 | convolution fusion | flops 4298637312 | bytes 17831944 | tf_op jit(solution)/shard_map/dot_general | solution.py:49
  147.9 39.9 %all-reduce = (f32[]{:T(128)}, f32[]{:T(128)}) all-reduce(f32[]{:T(128)} %get-tuple-element.3, f32[]{:T(128)} %get-tuple-element.2), channel_id=1, replica_groups=mesh['row'=8,'col'=4] {'row','col'}, use_global_device_ids=true, to_apply=%region_1.2 | all-reduce | flops 2 | bytes 16 | tf_op jit(solution)/shard_map/psum | solution.py:54
  190.3 3.2 %fusion.3 = bf16[512,1024]{1,0:T(8,128)(2,1)} fusion(f32[512,1024]{1,0:T(8,128)S(1)} %copy-done.1, bf16[512,1024]{1,0:T(8,128)(2,1)S(1)} %copy-done, f32[512,1024]{1,0:T(8,128)} %get-tuple-element.10, pred[]{:T(512)S(6)} %gt.3), kind=kLoop, calls=%fused_computation.7 | loop fusion | flops 3670016 | bytes 6291457 | tf_op jit(solution)/shard_map/convert_element_type | solution.py:60
  193.4 1.2 maximum_multiply_fusion
  (3 shorter events, 0.0 us)
Async XLA Ops:
  7.2 128.8 %all-gather.2.cloned.1.call-start = ((), (), s32[]{:S(2)}) async-start(), calls=%async_computation | async-start | bytes 9437184 | tf_op jit(solution)/shard_map/all_gather | solution.py:41
  9.4 26.4 %collective-permute-start = (bf16[1,512,1024]{1,2,0:T(8,128)(2,1)S(1)}, bf16[1,512,1024]{1,2,0:T(8,128)(2,1)}, u32[]{:S(2)}, u32[]{:S(2)}) collective-permute-start(bf16[1,512,1024]{1,2,0:T(8,128)(2,1)S(1)} %bitcast.12), channel_id=1, source_target_pairs={{0,1},{1,0},{2,3},{3,2},{4,5},{5,4},{6,7},{7,6},{8,9},{9,8},{10,11... | collective-permute-start | bytes 3145736 | tf_op jit(solution)/shard_map/ppermute | solution.py:19
  37.1 4.3 %copy-start.2 = (s32[8,16]{1,0:T(8,128)S(1)}, s32[8,16]{1,0:T(8,128)}, u32[]{:S(2)}) copy-start(s32[8,16]{1,0:T(8,128)} %param.3) | copy-start | bytes 1540
  38.6 93.0 %collective-permute-start.1 = (bf16[2,512,1024]{1,2,0:T(8,128)(2,1)}, bf16[2,512,1024]{1,2,0:T(8,128)(2,1)}, u32[]{:S(2)}, u32[]{:S(2)}) collective-permute-start(bf16[2,512,1024]{1,2,0:T(8,128)(2,1)} %pad_maximum_fusion.1), channel_id=1, source_target_pairs={{0,2},{1,3},{2,0},{3,1},{4,6},{5,7},{6,4},{7,5},{8,10},{9,11},{10,... | collective-permute-start | bytes 6291464 | tf_op jit(solution)/shard_map/ppermute | solution.py:19
  133.5 2.5 %copy-start = (bf16[512,1024]{1,0:T(8,128)(2,1)S(1)}, bf16[512,1024]{1,0:T(8,128)(2,1)}, u32[]{:S(2)}) copy-start(bf16[512,1024]{1,0:T(8,128)(2,1)} %param.2) | copy-start | bytes 3145732
  133.5 3.3 %copy-start.1 = (f32[512,1024]{1,0:T(8,128)S(1)}, f32[512,1024]{1,0:T(8,128)}, u32[]{:S(2)}) copy-start(f32[512,1024]{1,0:T(8,128)} %reshape.20) | copy-start | bytes 6291460
Sparse Core Ops, SparseCore 0:
  9.9 57.0 all-gather.1
